TPU v7x, 256 devices: a whole 4x4x8 slice. The times are simulated.
256 devices in a mesh: req: 16 (over x, y), seq: 16 (over z, core).
Axes of the slice: x: 4, y: 4, z: 8, core: 2. Of those that a mesh axis runs over, the one named last changes fastest.
Arguments:
- store: bfloat16 [144, 16, 56, 1024], P('req', 'seq'), may hold values from -6 to 6
- passage_owner: int32 [16, 256, 1], P(None, 'seq'), may hold values from 0 to 15; in each aligned block of 16 rows (0 to 15, 16 to 31, ..., all dimensions but the last counted through in order) at most 2 rows name the same one
- passage_slot: int32 [16, 256], P(None, 'seq'), may hold values from 0 to 8
- sel_pos: int32 [16, 1792], P('req'), may hold values from 0 to 14335, as said below
- queries: bfloat16 [16, 1792, 2048], P('req', 'seq'), may hold values from -512 to 512
- new_kv: bfloat16 [16, 1792, 1024], P('req', 'seq'), may hold values from -6 to 6
Outputs:
- blended_kv: bfloat16 [16, 14336, 1024], P('req', 'seq')
- deviation: float32 [16, 1792, 4], P('req', 'seq')
- attended: bfloat16 [16, 1792, 2048], P('req', 'seq')
Inputs may be any that keep to these rules, and one draw needn't show every extreme that they name: `passage_owner`: within the 16 pieces of one request's position block no owner is named more than 2 times, and some block names one owner exactly 2 times. `sel_pos`: entries b * 112 to (b + 1) * 112 - 1 of a request are distinct positions of block b, between b * 896 and (b + 1) * 896 - 1.
All inputs are finite; a program needn't handle non-finite values.
Results may differ from a plain program's by a relative error of at most 0.005.
Values may be sent and summed in bfloat16 or wider, within the bound.
A program may use at most 128 MiB of HBM per device.

v0:
```python
import jax
import jax.numpy as jnp
from jax import lax
from jax.sharding import PartitionSpec as P

HEAD_DIM = 128
KV_HEADS = 4
PASSAGE = 56
PASSAGES_DEV = 16
TOK_DEV = 896
SEL_DEV = 112
Q_WIDTH = 2048
KV_WIDTH = 1024
GROUP = 4


def update(carry_state, query_rows, query_pos, key_rows, value_rows, key_pos):
    running_max, weight_sum, summed = carry_state
    row_count = query_rows.shape[0]
    score_scale = HEAD_DIM ** (-0.5)
    query_split = query_rows.reshape(row_count, KV_HEADS, GROUP, HEAD_DIM)
    scores = (
        jnp.einsum("qkgd,pkd->qkgp", query_split, key_rows, preferred_element_type=jnp.float32)
        * score_scale
    )
    visible = key_pos[None, None, None, :] <= query_pos[:, None, None, None]
    scores = jnp.where(visible, scores, -1e30)
    new_max = jnp.maximum(running_max, jnp.max(scores, axis=-1))
    weights = jnp.where(visible, jnp.exp(scores - new_max[..., None]), 0.0)
    rescale = jnp.exp(running_max - new_max)
    weight_sum = weight_sum * rescale + jnp.sum(weights, axis=-1)
    product = jnp.einsum(
        "qkgp,pkd->qkgd",
        weights.astype(jnp.bfloat16),
        value_rows,
        preferred_element_type=jnp.float32,
    )
    summed = summed * rescale[..., None] + product
    return (new_max, weight_sum, summed)


def fold_attention(groups, blended):
    initial = []
    for query_rows, query_pos in groups:
        row_count = query_rows.shape[0]
        initial.append(
            (
                jnp.full((row_count, KV_HEADS, GROUP), -1e30, jnp.float32),
                jnp.zeros((row_count, KV_HEADS, GROUP), jnp.float32),
                jnp.zeros((row_count, KV_HEADS, GROUP, HEAD_DIM), jnp.float32),
            )
        )
    carry_all = tuple(initial)
    piece = lax.all_gather(blended, "seq", axis=0, tiled=True)
    absorb_row_count = piece.shape[0]
    block_rows = 512

    def take_block(state_all, step_index):
        key_part = lax.dynamic_slice_in_dim(piece, step_index * block_rows, block_rows, 0)
        first_pos = step_index * block_rows
        key_rows = key_part[:, : KV_HEADS * HEAD_DIM].reshape(block_rows, KV_HEADS, HEAD_DIM)
        value_rows = key_part[:, KV_HEADS * HEAD_DIM :].reshape(block_rows, KV_HEADS, HEAD_DIM)
        key_pos = first_pos + jnp.arange(block_rows, dtype=jnp.int32)
        updated = []
        for (query_rows, query_pos), carry_state in zip(groups, state_all):
            updated.append(
                lax.cond(
                    first_pos <= jnp.max(query_pos),
                    lambda state_in: update(
                        state_in, query_rows, query_pos, key_rows, value_rows, key_pos
                    ),
                    lambda state_in: state_in,
                    carry_state,
                )
            )
        return (tuple(updated), None)

    carry_all, _ = lax.scan(take_block, carry_all, jnp.arange(absorb_row_count // block_rows))
    finished = []
    for (query_rows, query_pos), carry_state in zip(groups, carry_all):
        row_count = query_rows.shape[0]
        output_rows = carry_state[2] / carry_state[1][..., None]
        finished.append(output_rows.reshape(row_count, Q_WIDTH).astype(jnp.bfloat16))
    return finished


def body(store, passage_owner, passage_slot, sel_pos, queries, new_kv):
    req_index = lax.axis_index("req")
    seq_index = lax.axis_index("seq")
    owner_table = passage_owner[:, :, 0]
    my_owner = lax.dynamic_index_in_dim(owner_table, req_index, 0, keepdims=False)
    store_shard = store[:, 0]
    req_count = owner_table.shape[0]
    owner_cap = max(2, (2 * PASSAGES_DEV + req_count - 1) // req_count)
    earlier = jnp.arange(PASSAGES_DEV)[:, None] > jnp.arange(PASSAGES_DEV)[None, :]
    same_owner = owner_table[:, :, None] == owner_table[:, None, :]
    rank_table = jnp.sum(same_owner & earlier[None], axis=2)
    slot_hit = (owner_table == req_index)[:, :, None] & (
        rank_table[:, :, None] == jnp.arange(owner_cap)[None, None, :]
    )
    send_slot = jnp.sum(jnp.where(slot_hit, passage_slot[:, :, None], 0), axis=1)
    outgoing = jnp.take(store_shard, send_slot.reshape(-1), axis=0)
    outgoing = outgoing.reshape(req_count, owner_cap, PASSAGE, KV_WIDTH)
    incoming = lax.all_to_all(outgoing, "req", split_axis=0, concat_axis=0, tiled=True)
    my_rank = lax.dynamic_index_in_dim(rank_table, req_index, 0, keepdims=False)
    flat_slot = my_owner * owner_cap + my_rank
    cached = jnp.take(incoming.reshape(req_count * owner_cap, PASSAGE, KV_WIDTH), flat_slot, axis=0)
    cached = cached.reshape(TOK_DEV, KV_WIDTH)
    all_pos = sel_pos[0]
    own_pos = lax.dynamic_slice_in_dim(all_pos, seq_index * SEL_DEV, SEL_DEV)
    offset = own_pos - seq_index * TOK_DEV
    fresh_rows = new_kv[0]
    picked = jnp.take(cached, offset, axis=0)
    blended = cached.at[offset].set(fresh_rows)
    difference = fresh_rows.astype(jnp.float32) - picked.astype(jnp.float32)
    squared = (difference * difference).reshape(SEL_DEV, 2, KV_HEADS, HEAD_DIM)
    deviation = jnp.sum(squared, axis=(1, 3))
    query_local = queries[0]
    attended = fold_attention([(query_local, own_pos)], blended)[0]
    return (blended[None], deviation[None], attended[None])


def solution(mesh):
    placed = (
        P("req", "seq", None, None),
        P(None, "seq", None),
        P(None, "seq"),
        P("req", None),
        P("req", "seq", None),
        P("req", "seq", None),
    )
    return jax.shard_map(
        body,
        mesh=mesh,
        in_specs=placed,
        out_specs=(P("req", "seq", None), P("req", "seq", None), P("req", "seq", None)),
        check_vma=False,
    )
```

profile of v0, /device:TPU:225, one launch (start us, length us, event | category | flops | bytes accessed | tf_op | source)
XLA Modules:
  0.0 505.5 jit_solution(7057776193855823319)
XLA Ops:
  10.3 2.6 gather_fusion
  13.0 4.2 broadcast_select_fusion
  17.2 6.8 %all-to-all-start = ((bf16[16,2,56,1024]{3,2,1,0:T(8,128)(2,1)}), bf16[16,2,56,1024]{3,2,1,0:T(8,128)(2,1)}, u32[]{:S(2)}, u32[]{:S(2)}) async-start(bf16[16,2,56,1024]{3,2,1,0:T(8,128)(2,1)} %broadcast_select_fusion), calls=%async_computation | async-start | bytes 7340032 | tf_op jit(solution)/shard_map/all_to_all | solution.py:104
  27.0 45.7 %all-to-all-done = bf16[16,2,56,1024]{3,2,1,0:T(8,128)(2,1)} async-done(((bf16[16,2,56,1024]{3,2,1,0:T(8,128)(2,1)}), bf16[16,2,56,1024]{3,2,1,0:T(8,128)(2,1)}, u32[]{:S(2)}, u32[]{:S(2)}) %all-to-all-start) | async-done | bytes 3670048 | tf_op jit(solution)/shard_map/all_to_all | solution.py:104
  72.7 3.9 gather_fusion.1
  79.3 2.1 scatter_custom_fusion
  84.1 158.5 %all-gather.2.cloned.1.call-done = bf16[14336,1024]{1,0:T(8,128)(2,1)} async-done(((bf16[896,1024]{1,0:T(8,128)(2,1)}), bf16[14336,1024]{1,0:T(8,128)(2,1)}) %all-gather.2.cloned.1.call-update) | async-done | bytes 29360144 | tf_op jit(solution)/shard_map/all_gather | solution.py:54
  242.6 35.1 %copy.27 = bf16[14336,1024]{0,1:T(8,128)(2,1)} copy(bf16[14336,1024]{1,0:T(8,128)(2,1)} %all-gather.2.cloned.1.call-done) | data formatting | bytes 58720256 | tf_op jit(solution)/shard_map/while | solution.py:78
  277.8 219.3 %while.15 = (s32[]{:T(128)}, f32[112,4,4]{0,2,1:T(4,128)S(1)}, f32[112,4,4]{0,2,1:T(4,128)S(1)}, f32[112,4,4,128]{3,0,2,1:T(8,128)S(1)}, s32[28]{0:T(128)S(1)}, ...) while((s32[]{:T(128)}, f32[112,4,4]{0,2,1:T(4,128)S(1)}, ...), condition=%wide.region_10.11_spmd, body=%wide.region_5.10_spmd.sunk | while | flops 482209792 | bytes 17720068 | solution.py:78
  279.7 5.9 %conditional.2 = ((f32[112,4,4]{0,2,1:T(4,128)S(1)}, f32[112,4,4]{0,2,1:T(4,128)S(1)}, f32[112,4,4,128]{3,0,2,1:T(8,128)S(1)})) conditional(s32[]{:T(128)} %convert_element_type.61, (f32[112,4,4]{0,2,1:T(4,128)S(1)}, f32[112,4,4]{0,2,1:T(4,128)S(1)}, f32[112,4,4,128]{3,0,2,1:T(8,128)S(1)}) %tuple.51, (s32[]{:T(128)}, s32[512]{0:T(512)S(1)}, ...), branch_computations={%region_6.6_spmd, %region_7.9_spmd} | conditional | flops 482209792 | bytes 17717786 | solution.py:67
  279.7 1.9 fusion.25
  287.5 5.9 %conditional.2 = ((f32[112,4,4]{0,2,1:T(4,128)S(1)}, f32[112,4,4]{0,2,1:T(4,128)S(1)}, f32[112,4,4,128]{3,0,2,1:T(8,128)S(1)})) conditional(s32[]{:T(128)} %convert_element_type.61, (f32[112,4,4]{0,2,1:T(4,128)S(1)}, f32[112,4,4]{0,2,1:T(4,128)S(1)}, f32[112,4,4,128]{3,0,2,1:T(8,128)S(1)}) %tuple.51, (s32[]{:T(128)}, s32[512]{0:T(512)S(1)}, ...), branch_computations={%region_6.6_spmd, %region_7.9_spmd} | conditional | flops 482209792 | bytes 17717786 | solution.py:67
  287.5 1.9 fusion.25
  295.4 5.9 %conditional.2 = ((f32[112,4,4]{0,2,1:T(4,128)S(1)}, f32[112,4,4]{0,2,1:T(4,128)S(1)}, f32[112,4,4,128]{3,0,2,1:T(8,128)S(1)})) conditional(s32[]{:T(128)} %convert_element_type.61, (f32[112,4,4]{0,2,1:T(4,128)S(1)}, f32[112,4,4]{0,2,1:T(4,128)S(1)}, f32[112,4,4,128]{3,0,2,1:T(8,128)S(1)}) %tuple.51, (s32[]{:T(128)}, s32[512]{0:T(512)S(1)}, ...), branch_computations={%region_6.6_spmd, %region_7.9_spmd} | conditional | flops 482209792 | bytes 17717786 | solution.py:67
  295.4 1.9 fusion.25
  303.2 5.9 %conditional.2 = ((f32[112,4,4]{0,2,1:T(4,128)S(1)}, f32[112,4,4]{0,2,1:T(4,128)S(1)}, f32[112,4,4,128]{3,0,2,1:T(8,128)S(1)})) conditional(s32[]{:T(128)} %convert_element_type.61, (f32[112,4,4]{0,2,1:T(4,128)S(1)}, f32[112,4,4]{0,2,1:T(4,128)S(1)}, f32[112,4,4,128]{3,0,2,1:T(8,128)S(1)}) %tuple.51, (s32[]{:T(128)}, s32[512]{0:T(512)S(1)}, ...), branch_computations={%region_6.6_spmd, %region_7.9_spmd} | conditional | flops 482209792 | bytes 17717786 | solution.py:67
  303.2 1.9 fusion.25
  311.0 5.9 %conditional.2 = ((f32[112,4,4]{0,2,1:T(4,128)S(1)}, f32[112,4,4]{0,2,1:T(4,128)S(1)}, f32[112,4,4,128]{3,0,2,1:T(8,128)S(1)})) conditional(s32[]{:T(128)} %convert_element_type.61, (f32[112,4,4]{0,2,1:T(4,128)S(1)}, f32[112,4,4]{0,2,1:T(4,128)S(1)}, f32[112,4,4,128]{3,0,2,1:T(8,128)S(1)}) %tuple.51, (s32[]{:T(128)}, s32[512]{0:T(512)S(1)}, ...), branch_computations={%region_6.6_spmd, %region_7.9_spmd} | conditional | flops 482209792 | bytes 17717786 | solution.py:67
  311.0 1.9 fusion.25
  318.9 5.9 %conditional.2 = ((f32[112,4,4]{0,2,1:T(4,128)S(1)}, f32[112,4,4]{0,2,1:T(4,128)S(1)}, f32[112,4,4,128]{3,0,2,1:T(8,128)S(1)})) conditional(s32[]{:T(128)} %convert_element_type.61, (f32[112,4,4]{0,2,1:T(4,128)S(1)}, f32[112,4,4]{0,2,1:T(4,128)S(1)}, f32[112,4,4,128]{3,0,2,1:T(8,128)S(1)}) %tuple.51, (s32[]{:T(128)}, s32[512]{0:T(512)S(1)}, ...), branch_computations={%region_6.6_spmd, %region_7.9_spmd} | conditional | flops 482209792 | bytes 17717786 | solution.py:67
  318.9 1.9 fusion.25
  326.7 5.9 %conditional.2 = ((f32[112,4,4]{0,2,1:T(4,128)S(1)}, f32[112,4,4]{0,2,1:T(4,128)S(1)}, f32[112,4,4,128]{3,0,2,1:T(8,128)S(1)})) conditional(s32[]{:T(128)} %convert_element_type.61, (f32[112,4,4]{0,2,1:T(4,128)S(1)}, f32[112,4,4]{0,2,1:T(4,128)S(1)}, f32[112,4,4,128]{3,0,2,1:T(8,128)S(1)}) %tuple.51, (s32[]{:T(128)}, s32[512]{0:T(512)S(1)}, ...), branch_computations={%region_6.6_spmd, %region_7.9_spmd} | conditional | flops 482209792 | bytes 17717786 | solution.py:67
  326.7 1.9 fusion.25
  334.5 5.9 %conditional.2 = ((f32[112,4,4]{0,2,1:T(4,128)S(1)}, f32[112,4,4]{0,2,1:T(4,128)S(1)}, f32[112,4,4,128]{3,0,2,1:T(8,128)S(1)})) conditional(s32[]{:T(128)} %convert_element_type.61, (f32[112,4,4]{0,2,1:T(4,128)S(1)}, f32[112,4,4]{0,2,1:T(4,128)S(1)}, f32[112,4,4,128]{3,0,2,1:T(8,128)S(1)}) %tuple.51, (s32[]{:T(128)}, s32[512]{0:T(512)S(1)}, ...), branch_computations={%region_6.6_spmd, %region_7.9_spmd} | conditional | flops 482209792 | bytes 17717786 | solution.py:67
  334.6 1.9 fusion.25
  342.4 5.9 %conditional.2 = ((f32[112,4,4]{0,2,1:T(4,128)S(1)}, f32[112,4,4]{0,2,1:T(4,128)S(1)}, f32[112,4,4,128]{3,0,2,1:T(8,128)S(1)})) conditional(s32[]{:T(128)} %convert_element_type.61, (f32[112,4,4]{0,2,1:T(4,128)S(1)}, f32[112,4,4]{0,2,1:T(4,128)S(1)}, f32[112,4,4,128]{3,0,2,1:T(8,128)S(1)}) %tuple.51, (s32[]{:T(128)}, s32[512]{0:T(512)S(1)}, ...), branch_computations={%region_6.6_spmd, %region_7.9_spmd} | conditional | flops 482209792 | bytes 17717786 | solution.py:67
  342.4 1.9 fusion.25
  350.2 5.9 %conditional.2 = ((f32[112,4,4]{0,2,1:T(4,128)S(1)}, f32[112,4,4]{0,2,1:T(4,128)S(1)}, f32[112,4,4,128]{3,0,2,1:T(8,128)S(1)})) conditional(s32[]{:T(128)} %convert_element_type.61, (f32[112,4,4]{0,2,1:T(4,128)S(1)}, f32[112,4,4]{0,2,1:T(4,128)S(1)}, f32[112,4,4,128]{3,0,2,1:T(8,128)S(1)}) %tuple.51, (s32[]{:T(128)}, s32[512]{0:T(512)S(1)}, ...), branch_computations={%region_6.6_spmd, %region_7.9_spmd} | conditional | flops 482209792 | bytes 17717786 | solution.py:67
  350.2 1.9 fusion.25
  358.0 5.9 %conditional.2 = ((f32[112,4,4]{0,2,1:T(4,128)S(1)}, f32[112,4,4]{0,2,1:T(4,128)S(1)}, f32[112,4,4,128]{3,0,2,1:T(8,128)S(1)})) conditional(s32[]{:T(128)} %convert_element_type.61, (f32[112,4,4]{0,2,1:T(4,128)S(1)}, f32[112,4,4]{0,2,1:T(4,128)S(1)}, f32[112,4,4,128]{3,0,2,1:T(8,128)S(1)}) %tuple.51, (s32[]{:T(128)}, s32[512]{0:T(512)S(1)}, ...), branch_computations={%region_6.6_spmd, %region_7.9_spmd} | conditional | flops 482209792 | bytes 17717786 | solution.py:67
  358.1 1.9 fusion.25
  365.9 5.9 %conditional.2 = ((f32[112,4,4]{0,2,1:T(4,128)S(1)}, f32[112,4,4]{0,2,1:T(4,128)S(1)}, f32[112,4,4,128]{3,0,2,1:T(8,128)S(1)})) conditional(s32[]{:T(128)} %convert_element_type.61, (f32[112,4,4]{0,2,1:T(4,128)S(1)}, f32[112,4,4]{0,2,1:T(4,128)S(1)}, f32[112,4,4,128]{3,0,2,1:T(8,128)S(1)}) %tuple.51, (s32[]{:T(128)}, s32[512]{0:T(512)S(1)}, ...), branch_computations={%region_6.6_spmd, %region_7.9_spmd} | conditional | flops 482209792 | bytes 17717786 | solution.py:67
  365.9 1.9 fusion.25
  373.7 5.9 %conditional.2 = ((f32[112,4,4]{0,2,1:T(4,128)S(1)}, f32[112,4,4]{0,2,1:T(4,128)S(1)}, f32[112,4,4,128]{3,0,2,1:T(8,128)S(1)})) conditional(s32[]{:T(128)} %convert_element_type.61, (f32[112,4,4]{0,2,1:T(4,128)S(1)}, f32[112,4,4]{0,2,1:T(4,128)S(1)}, f32[112,4,4,128]{3,0,2,1:T(8,128)S(1)}) %tuple.51, (s32[]{:T(128)}, s32[512]{0:T(512)S(1)}, ...), branch_computations={%region_6.6_spmd, %region_7.9_spmd} | conditional | flops 482209792 | bytes 17717786 | solution.py:67
  373.7 1.9 fusion.25
  381.5 5.9 %conditional.2 = ((f32[112,4,4]{0,2,1:T(4,128)S(1)}, f32[112,4,4]{0,2,1:T(4,128)S(1)}, f32[112,4,4,128]{3,0,2,1:T(8,128)S(1)})) conditional(s32[]{:T(128)} %convert_element_type.61, (f32[112,4,4]{0,2,1:T(4,128)S(1)}, f32[112,4,4]{0,2,1:T(4,128)S(1)}, f32[112,4,4,128]{3,0,2,1:T(8,128)S(1)}) %tuple.51, (s32[]{:T(128)}, s32[512]{0:T(512)S(1)}, ...), branch_computations={%region_6.6_spmd, %region_7.9_spmd} | conditional | flops 482209792 | bytes 17717786 | solution.py:67
  381.6 1.9 fusion.25
  389.4 5.9 %conditional.2 = ((f32[112,4,4]{0,2,1:T(4,128)S(1)}, f32[112,4,4]{0,2,1:T(4,128)S(1)}, f32[112,4,4,128]{3,0,2,1:T(8,128)S(1)})) conditional(s32[]{:T(128)} %convert_element_type.61, (f32[112,4,4]{0,2,1:T(4,128)S(1)}, f32[112,4,4]{0,2,1:T(4,128)S(1)}, f32[112,4,4,128]{3,0,2,1:T(8,128)S(1)}) %tuple.51, (s32[]{:T(128)}, s32[512]{0:T(512)S(1)}, ...), branch_computations={%region_6.6_spmd, %region_7.9_spmd} | conditional | flops 482209792 | bytes 17717786 | solution.py:67
  389.4 1.9 fusion.25
  397.2 5.9 %conditional.2 = ((f32[112,4,4]{0,2,1:T(4,128)S(1)}, f32[112,4,4]{0,2,1:T(4,128)S(1)}, f32[112,4,4,128]{3,0,2,1:T(8,128)S(1)})) conditional(s32[]{:T(128)} %convert_element_type.61, (f32[112,4,4]{0,2,1:T(4,128)S(1)}, f32[112,4,4]{0,2,1:T(4,128)S(1)}, f32[112,4,4,128]{3,0,2,1:T(8,128)S(1)}) %tuple.51, (s32[]{:T(128)}, s32[512]{0:T(512)S(1)}, ...), branch_computations={%region_6.6_spmd, %region_7.9_spmd} | conditional | flops 482209792 | bytes 17717786 | solution.py:67
  397.2 1.9 fusion.25
  405.0 5.9 %conditional.2 = ((f32[112,4,4]{0,2,1:T(4,128)S(1)}, f32[112,4,4]{0,2,1:T(4,128)S(1)}, f32[112,4,4,128]{3,0,2,1:T(8,128)S(1)})) conditional(s32[]{:T(128)} %convert_element_type.61, (f32[112,4,4]{0,2,1:T(4,128)S(1)}, f32[112,4,4]{0,2,1:T(4,128)S(1)}, f32[112,4,4,128]{3,0,2,1:T(8,128)S(1)}) %tuple.51, (s32[]{:T(128)}, s32[512]{0:T(512)S(1)}, ...), branch_computations={%region_6.6_spmd, %region_7.9_spmd} | conditional | flops 482209792 | bytes 17717786 | solution.py:67
  405.1 1.9 fusion.25
  412.9 5.9 %conditional.2 = ((f32[112,4,4]{0,2,1:T(4,128)S(1)}, f32[112,4,4]{0,2,1:T(4,128)S(1)}, f32[112,4,4,128]{3,0,2,1:T(8,128)S(1)})) conditional(s32[]{:T(128)} %convert_element_type.61, (f32[112,4,4]{0,2,1:T(4,128)S(1)}, f32[112,4,4]{0,2,1:T(4,128)S(1)}, f32[112,4,4,128]{3,0,2,1:T(8,128)S(1)}) %tuple.51, (s32[]{:T(128)}, s32[512]{0:T(512)S(1)}, ...), branch_computations={%region_6.6_spmd, %region_7.9_spmd} | conditional | flops 482209792 | bytes 17717786 | solution.py:67
  412.9 1.9 fusion.25
  420.7 5.9 %conditional.2 = ((f32[112,4,4]{0,2,1:T(4,128)S(1)}, f32[112,4,4]{0,2,1:T(4,128)S(1)}, f32[112,4,4,128]{3,0,2,1:T(8,128)S(1)})) conditional(s32[]{:T(128)} %convert_element_type.61, (f32[112,4,4]{0,2,1:T(4,128)S(1)}, f32[112,4,4]{0,2,1:T(4,128)S(1)}, f32[112,4,4,128]{3,0,2,1:T(8,128)S(1)}) %tuple.51, (s32[]{:T(128)}, s32[512]{0:T(512)S(1)}, ...), branch_computations={%region_6.6_spmd, %region_7.9_spmd} | conditional | flops 482209792 | bytes 17717786 | solution.py:67
  420.7 1.9 fusion.25
  428.5 5.9 %conditional.2 = ((f32[112,4,4]{0,2,1:T(4,128)S(1)}, f32[112,4,4]{0,2,1:T(4,128)S(1)}, f32[112,4,4,128]{3,0,2,1:T(8,128)S(1)})) conditional(s32[]{:T(128)} %convert_element_type.61, (f32[112,4,4]{0,2,1:T(4,128)S(1)}, f32[112,4,4]{0,2,1:T(4,128)S(1)}, f32[112,4,4,128]{3,0,2,1:T(8,128)S(1)}) %tuple.51, (s32[]{:T(128)}, s32[512]{0:T(512)S(1)}, ...), branch_computations={%region_6.6_spmd, %region_7.9_spmd} | conditional | flops 482209792 | bytes 17717786 | solution.py:67
  428.6 1.9 fusion.25
  436.4 5.9 %conditional.2 = ((f32[112,4,4]{0,2,1:T(4,128)S(1)}, f32[112,4,4]{0,2,1:T(4,128)S(1)}, f32[112,4,4,128]{3,0,2,1:T(8,128)S(1)})) conditional(s32[]{:T(128)} %convert_element_type.61, (f32[112,4,4]{0,2,1:T(4,128)S(1)}, f32[112,4,4]{0,2,1:T(4,128)S(1)}, f32[112,4,4,128]{3,0,2,1:T(8,128)S(1)}) %tuple.51, (s32[]{:T(128)}, s32[512]{0:T(512)S(1)}, ...), branch_computations={%region_6.6_spmd, %region_7.9_spmd} | conditional | flops 482209792 | bytes 17717786 | solution.py:67
  436.4 1.9 fusion.25
  444.2 5.9 %conditional.2 = ((f32[112,4,4]{0,2,1:T(4,128)S(1)}, f32[112,4,4]{0,2,1:T(4,128)S(1)}, f32[112,4,4,128]{3,0,2,1:T(8,128)S(1)})) conditional(s32[]{:T(128)} %convert_element_type.61, (f32[112,4,4]{0,2,1:T(4,128)S(1)}, f32[112,4,4]{0,2,1:T(4,128)S(1)}, f32[112,4,4,128]{3,0,2,1:T(8,128)S(1)}) %tuple.51, (s32[]{:T(128)}, s32[512]{0:T(512)S(1)}, ...), branch_computations={%region_6.6_spmd, %region_7.9_spmd} | conditional | flops 482209792 | bytes 17717786 | solution.py:67
  444.2 1.9 fusion.25
  452.0 5.9 %conditional.2 = ((f32[112,4,4]{0,2,1:T(4,128)S(1)}, f32[112,4,4]{0,2,1:T(4,128)S(1)}, f32[112,4,4,128]{3,0,2,1:T(8,128)S(1)})) conditional(s32[]{:T(128)} %convert_element_type.61, (f32[112,4,4]{0,2,1:T(4,128)S(1)}, f32[112,4,4]{0,2,1:T(4,128)S(1)}, f32[112,4,4,128]{3,0,2,1:T(8,128)S(1)}) %tuple.51, (s32[]{:T(128)}, s32[512]{0:T(512)S(1)}, ...), branch_computations={%region_6.6_spmd, %region_7.9_spmd} | conditional | flops 482209792 | bytes 17717786 | solution.py:67
  452.1 1.9 fusion.25
  459.9 5.9 %conditional.2 = ((f32[112,4,4]{0,2,1:T(4,128)S(1)}, f32[112,4,4]{0,2,1:T(4,128)S(1)}, f32[112,4,4,128]{3,0,2,1:T(8,128)S(1)})) conditional(s32[]{:T(128)} %convert_element_type.61, (f32[112,4,4]{0,2,1:T(4,128)S(1)}, f32[112,4,4]{0,2,1:T(4,128)S(1)}, f32[112,4,4,128]{3,0,2,1:T(8,128)S(1)}) %tuple.51, (s32[]{:T(128)}, s32[512]{0:T(512)S(1)}, ...), branch_computations={%region_6.6_spmd, %region_7.9_spmd} | conditional | flops 482209792 | bytes 17717786 | solution.py:67
  459.9 1.9 fusion.25
  467.7 5.9 %conditional.2 = ((f32[112,4,4]{0,2,1:T(4,128)S(1)}, f32[112,4,4]{0,2,1:T(4,128)S(1)}, f32[112,4,4,128]{3,0,2,1:T(8,128)S(1)})) conditional(s32[]{:T(128)} %convert_element_type.61, (f32[112,4,4]{0,2,1:T(4,128)S(1)}, f32[112,4,4]{0,2,1:T(4,128)S(1)}, f32[112,4,4,128]{3,0,2,1:T(8,128)S(1)}) %tuple.51, (s32[]{:T(128)}, s32[512]{0:T(512)S(1)}, ...), branch_computations={%region_6.6_spmd, %region_7.9_spmd} | conditional | flops 482209792 | bytes 17717786 | solution.py:67
  467.7 1.9 fusion.25
  475.5 5.9 %conditional.2 = ((f32[112,4,4]{0,2,1:T(4,128)S(1)}, f32[112,4,4]{0,2,1:T(4,128)S(1)}, f32[112,4,4,128]{3,0,2,1:T(8,128)S(1)})) conditional(s32[]{:T(128)} %convert_element_type.61, (f32[112,4,4]{0,2,1:T(4,128)S(1)}, f32[112,4,4]{0,2,1:T(4,128)S(1)}, f32[112,4,4,128]{3,0,2,1:T(8,128)S(1)}) %tuple.51, (s32[]{:T(128)}, s32[512]{0:T(512)S(1)}, ...), branch_computations={%region_6.6_spmd, %region_7.9_spmd} | conditional | flops 482209792 | bytes 17717786 | solution.py:67
  475.6 1.9 fusion.25
  483.4 5.9 %conditional.2 = ((f32[112,4,4]{0,2,1:T(4,128)S(1)}, f32[112,4,4]{0,2,1:T(4,128)S(1)}, f32[112,4,4,128]{3,0,2,1:T(8,128)S(1)})) conditional(s32[]{:T(128)} %convert_element_type.61, (f32[112,4,4]{0,2,1:T(4,128)S(1)}, f32[112,4,4]{0,2,1:T(4,128)S(1)}, f32[112,4,4,128]{3,0,2,1:T(8,128)S(1)}) %tuple.51, (s32[]{:T(128)}, s32[512]{0:T(512)S(1)}, ...), branch_computations={%region_6.6_spmd, %region_7.9_spmd} | conditional | flops 482209792 | bytes 17717786 | solution.py:67
  483.4 1.9 fusion.25
  491.2 5.8 %conditional.2 = ((f32[112,4,4]{0,2,1:T(4,128)S(1)}, f32[112,4,4]{0,2,1:T(4,128)S(1)}, f32[112,4,4,128]{3,0,2,1:T(8,128)S(1)})) conditional(s32[]{:T(128)} %convert_element_type.61, (f32[112,4,4]{0,2,1:T(4,128)S(1)}, f32[112,4,4]{0,2,1:T(4,128)S(1)}, f32[112,4,4,128]{3,0,2,1:T(8,128)S(1)}) %tuple.51, (s32[]{:T(128)}, s32[512]{0:T(512)S(1)}, ...), branch_computations={%region_6.6_spmd, %region_7.9_spmd} | conditional | flops 482209792 | bytes 17717786 | solution.py:67
  (354 shorter events, 143.4 us)
Async XLA Ops:
  7.2 3.2 copy-start
  17.2 55.5 %all-to-all-start = ((bf16[16,2,56,1024]{3,2,1,0:T(8,128)(2,1)}), bf16[16,2,56,1024]{3,2,1,0:T(8,128)(2,1)}, u32[]{:S(2)}, u32[]{:S(2)}) async-start(bf16[16,2,56,1024]{3,2,1,0:T(8,128)(2,1)} %broadcast_select_fusion), calls=%async_computation | async-start | bytes 7340032 | tf_op jit(solution)/shard_map/all_to_all | solution.py:104
  76.6 2.7 copy-start.4
  79.2 163.4 %all-gather.2.cloned.1.call-start = ((), (), s32[]{:S(2)}) async-start(), calls=%async_computation.1 | async-start | bytes 31195136 | tf_op jit(solution)/shard_map/all_gather | solution.py:54
  81.4 1.2 copy-start.2
  84.1 193.7 %copy-start.3 = (bf16[1,112,2048]{2,1,0:T(8,128)(2,1)S(1)}, bf16[1,112,2048]{2,1,0:T(8,128)(2,1)}, u32[]{:S(2)}) copy-start(bf16[1,112,2048]{2,1,0:T(8,128)(2,1)} %param.14) | copy-start | bytes 1376260
  497.0 1.6 copy-start.1
Sparse Core Ops, SparseCore 0:
  82.8 159.7 all-gather.1
where the time goes:
time: 508 us; the launch traced here: 506 us
  waiting for transfers between devices  204 us (40%)
  local copies, waits for them, and re-layouts  127 us (25%)
  matrix products  65.1 us (13%)
  other arithmetic  49.5 us (10%)
  loops' own time  38.6 us (8%)
  between operations  14.2 us (3%)
  starting transfers between devices  6.84 us (1%)
    all_gather x1, waiting for transfers between devices, fold_attention(): piece = lax.all_gather(blended, 'seq', axis=0, tiled=True)  159 us
    slice x28, local copies, waits for them, and re-layouts, take_block(): key_part[:, KV_HEADS * HEAD_DIM:].reshape(block_rows, KV_HEADS, HEAD_DIM)  52.1 us
    all_to_all x1, waiting for transfers between devices, body(): lax.all_to_all(outgoing, 'req', split_axis=0, concat_axis=0, tiled=True)  45.7 us
    dot_general x28, matrix products, update(): jnp.einsum('qkgp,pkd->qkgd', weights.astype(jnp.bfloat16), value_rows, pr...  42.1 us
    another operation x1, loops' own time, fold_attention(): lax.scan(take_block, carry_all, jnp.arange(absorb_row_count // block_rows))  36.9 us
    while x1, local copies, waits for them, and re-layouts, fold_attention(): lax.scan(take_block, carry_all, jnp.arange(absorb_row_count // block_rows))  35.1 us
    reduce_sum x28, other arithmetic, update(): weight_sum = weight_sum * rescale + jnp.sum(weights, axis=-1)  33.8 us
    dot_general x28, matrix products, update(): jnp.einsum('qkgd,pkd->qkgp', query_split, key_rows, preferred_element_typ...  23.1 us
  transfers between devices with their start and end apart: 2, of which 2 were waited for; matrix products, arithmetic and copies ran while one was open for 1% of the time, Pallas kernels for 0%

commit v1 on v0

--- a/solution.py
+++ b/solution.py
@@ -12,6 +12,17 @@
 Q_WIDTH = 2048
 KV_WIDTH = 1024
 GROUP = 4
+
+
+def in_blocks(x, dim, length):
+    before, after = (x.shape[:dim], x.shape[dim + 1 :])
+    return jnp.moveaxis(x.reshape(*before, length, -1, *after), dim, 0)
+
+
+def in_order(tiles, dim):
+    tiles = jnp.moveaxis(tiles, 0, dim)
+    shape = tiles.shape
+    return tiles.reshape(*shape[:dim], shape[dim] * shape[dim + 1], *shape[dim + 2 :])
 
 
 def update(carry_state, query_rows, query_pos, key_rows, value_rows, key_pos):
@@ -101,7 +112,14 @@
     send_slot = jnp.sum(jnp.where(slot_hit, passage_slot[:, :, None], 0), axis=1)
     outgoing = jnp.take(store_shard, send_slot.reshape(-1), axis=0)
     outgoing = outgoing.reshape(req_count, owner_cap, PASSAGE, KV_WIDTH)
-    incoming = lax.all_to_all(outgoing, "req", split_axis=0, concat_axis=0, tiled=True)
+    size, index = (lax.axis_size("req"), lax.axis_index("req"))
+    tiles = in_blocks(outgoing, 0, size)
+    finished_2 = [tiles[index]]
+    for turn in range(1, size):
+        sent = tiles[index ^ turn]
+        finished_2.append(lax.ppermute(sent, "req", [(i, i ^ turn) for i in range(size)]))
+    tiles = jnp.stack(finished_2)[index ^ jnp.arange(size)]
+    incoming = in_order(tiles, 0)
     my_rank = lax.dynamic_index_in_dim(rank_table, req_index, 0, keepdims=False)
     flat_slot = my_owner * owner_cap + my_rank
     cached = jnp.take(incoming.reshape(req_count * owner_cap, PASSAGE, KV_WIDTH), flat_slot, axis=0)

time: 508 us -> 528 us (1.039)
  starting transfers between devices: 6.84 us -> 28.2 us
  waiting for transfers between devices: 204 us -> 183 us
  local copies, waits for them, and re-layouts: 127 us -> 146 us
    all_to_all x1 -> x0, waiting for transfers between devices: 45.7 us -> none  [body(): lax.all_to_all(outgoing, 'req', split_axis=0, concat_axis=0, tiled=True)]
    ppermute x0 -> x15, waiting for transfers between devices: none -> 35.7 us  [body(): lax.ppermute(sent, 'req', [(i, i ^ turn) for i in range(size)])]
    ppermute x0 -> x15, starting transfers between devices: none -> 28.2 us  [body(): lax.ppermute(sent, 'req', [(i, i ^ turn) for i in range(size)])]
    all_gather x1, waiting for transfers between devices: 159 us -> 148 us  [fold_attention(): piece = lax.all_gather(blended, 'seq', axis=0, tiled=True)]
    unnamed x12 -> x28, local copies, waits for them, and re-layouts: 1.91 us -> 11.9 us
    all_to_all x1 -> x0, starting transfers between devices: 6.8 us -> none  [body(): lax.all_to_all(outgoing, 'req', split_axis=0, concat_axis=0, tiled=True)]
  transfers between devices with their start and end apart: 2 -> 16, of which waited for: 2 -> 7; matrix products, arithmetic and copies ran while one was open for 1% -> 3% of each run, Pallas kernels for 0% -> 0%
where the time goes in v1:
time: 528 us; the launch traced here: 525 us
  waiting for transfers between devices  183 us (35%)
  local copies, waits for them, and re-layouts  146 us (28%)
  matrix products  65.1 us (12%)
  other arithmetic  50.2 us (10%)
  loops' own time  38.6 us (7%)
  starting transfers between devices  28.2 us (5%)
  between operations  14.3 us (3%)
    all_gather x1, waiting for transfers between devices, fold_attention(): piece = lax.all_gather(blended, 'seq', axis=0, tiled=True)  148 us
    slice x28, local copies, waits for them, and re-layouts, take_block(): key_part[:, KV_HEADS * HEAD_DIM:].reshape(block_rows, KV_HEADS, HEAD_DIM)  52.1 us
    dot_general x28, matrix products, update(): jnp.einsum('qkgp,pkd->qkgd', weights.astype(jnp.bfloat16), value_rows, pr...  42 us
    another operation x1, loops' own time, fold_attention(): lax.scan(take_block, carry_all, jnp.arange(absorb_row_count // block_rows))  36.9 us
    ppermute x15, waiting for transfers between devices, body(): lax.ppermute(sent, 'req', [(i, i ^ turn) for i in range(size)])  35.7 us
    while x1, local copies, waits for them, and re-layouts, fold_attention(): lax.scan(take_block, carry_all, jnp.arange(absorb_row_count // block_rows))  35.6 us
    reduce_sum x28, other arithmetic, update(): weight_sum = weight_sum * rescale + jnp.sum(weights, axis=-1)  33.8 us
    ppermute x15, starting transfers between devices, body(): lax.ppermute(sent, 'req', [(i, i ^ turn) for i in range(size)])  28.2 us
  transfers between devices with their start and end apart: 16, of which 7 were waited for; matrix products, arithmetic and copies ran while one was open for 3% of the time, Pallas kernels for 0%

profile of v1, /device:TPU:225, one launch (start us, length us, event | category | flops | bytes accessed | tf_op | source)
XLA Modules:
  0.0 525.4 jit_solution(5510074260515025566)
XLA Ops:
  11.6 2.6 gather_fusion
  14.2 4.3 broadcast_select_fusion
  18.5 3.5 dynamic-slice_bitcast_fusion
  23.3 2.6 collective-permute-start.1
  29.5 4.8 collective-permute-start.5
  35.0 10.9 %collective-permute-done.1 = bf16[1,2,56,1024]{3,2,1,0:T(8,128)(2,1)S(1)} collective-permute-done((bf16[1,2,56,1024]{3,2,1,0:T(8,128)(2,1)}, bf16[1,2,56,1024]{3,2,1,0:T(8,128)(2,1)S(1)}, u32[]{:S(2)}, u32[]{:S(2)}) %collective-permute-start.1) | collective-permute-done | bytes 229408 | tf_op jit(solution)/shard_map/ppermute | solution.py:120
  47.5 2.5 collective-permute-start.7
  51.3 6.3 %collective-permute-start.9 = (bf16[1,2,56,1024]{3,2,1,0:T(8,128)(2,1)S(1)}, bf16[1,2,56,1024]{3,2,1,0:T(8,128)(2,1)S(1)}, u32[]{:S(2)}, u32[]{:S(2)}) collective-permute-start(bf16[1,2,56,1024]{3,2,1,0:T(8,128)(2,1)S(1)} %get-tuple-element.243), channel_id=1, source_target_pairs={{0,160},{16,176},{32,128},{48,144},{64,224},{80,240},{96,192},{112... | collective-permute-start | bytes 688136 | tf_op jit(solution)/shard_map/ppermute | solution.py:120
  62.6 5.9 %collective-permute-start.13 = (bf16[1,2,56,1024]{3,2,1,0:T(8,128)(2,1)S(1)}, bf16[1,2,56,1024]{3,2,1,0:T(8,128)(2,1)S(1)}, u32[]{:S(2)}, u32[]{:S(2)}) collective-permute-start(bf16[1,2,56,1024]{3,2,1,0:T(8,128)(2,1)S(1)} %get-tuple-element.239), channel_id=1, source_target_pairs={{0,224},{16,240},{32,192},{48,208},{64,160},{80,176},{96,128},{112... | collective-permute-start | bytes 688136 | tf_op jit(solution)/shard_map/ppermute | solution.py:120
  70.5 5.0 collective-permute-done.10
  76.2 3.6 collective-permute-done.11
  80.6 3.0 collective-permute-done.12
  84.3 4.4 collective-permute-done.13
  89.4 8.7 %collective-permute-done.14 = bf16[1,2,56,1024]{3,2,1,0:T(8,128)(2,1)S(1)} collective-permute-done((bf16[1,2,56,1024]{3,2,1,0:T(8,128)(2,1)S(1)}, bf16[1,2,56,1024]{3,2,1,0:T(8,128)(2,1)S(1)}, u32[]{:S(2)}, u32[]{:S(2)}) %collective-permute-start.14) | collective-permute-done | bytes 229408 | tf_op jit(solution)/shard_map/ppermute | solution.py:120
  98.8 4.7 gather_fusion.1
  103.5 4.1 gather_fusion.2
  110.2 2.3 scatter_custom_fusion
  115.2 147.5 %all-gather.2.cloned.1.call-done = bf16[14336,1024]{1,0:T(8,128)(2,1)} async-done(((bf16[896,1024]{1,0:T(8,128)(2,1)}), bf16[14336,1024]{1,0:T(8,128)(2,1)}) %all-gather.2.cloned.1.call-update) | async-done | bytes 29360144 | tf_op jit(solution)/shard_map/all_gather | solution.py:65
  262.7 35.6 %copy.27 = bf16[14336,1024]{0,1:T(8,128)(2,1)} copy(bf16[14336,1024]{1,0:T(8,128)(2,1)} %all-gather.2.cloned.1.call-done) | data formatting | bytes 58720256 | tf_op jit(solution)/shard_map/while | solution.py:89
  298.5 218.4 %while.15 = (s32[]{:T(128)}, f32[112,4,4]{0,2,1:T(4,128)S(1)}, f32[112,4,4]{0,2,1:T(4,128)S(1)}, f32[112,4,4,128]{3,0,2,1:T(8,128)S(1)}, s32[28]{0:T(128)S(1)}, ...) while((s32[]{:T(128)}, f32[112,4,4]{0,2,1:T(4,128)S(1)}, ...), condition=%wide.region_10.11_spmd, body=%wide.region_5.10_spmd.sunk | while | flops 482209792 | bytes 17720068 | solution.py:89
  300.4 5.9 %conditional.2 = ((f32[112,4,4]{0,2,1:T(4,128)S(1)}, f32[112,4,4]{0,2,1:T(4,128)S(1)}, f32[112,4,4,128]{3,0,2,1:T(8,128)S(1)})) conditional(s32[]{:T(128)} %convert_element_type.61, (f32[112,4,4]{0,2,1:T(4,128)S(1)}, f32[112,4,4]{0,2,1:T(4,128)S(1)}, f32[112,4,4,128]{3,0,2,1:T(8,128)S(1)}) %tuple.67, (s32[]{:T(128)}, s32[512]{0:T(512)S(1)}, ...), branch_computations={%region_6.6_spmd, %region_7.9_spmd} | conditional | flops 482209792 | bytes 17717786 | solution.py:78
  300.4 1.9 fusion.26
  308.2 5.9 %conditional.2 = ((f32[112,4,4]{0,2,1:T(4,128)S(1)}, f32[112,4,4]{0,2,1:T(4,128)S(1)}, f32[112,4,4,128]{3,0,2,1:T(8,128)S(1)})) conditional(s32[]{:T(128)} %convert_element_type.61, (f32[112,4,4]{0,2,1:T(4,128)S(1)}, f32[112,4,4]{0,2,1:T(4,128)S(1)}, f32[112,4,4,128]{3,0,2,1:T(8,128)S(1)}) %tuple.67, (s32[]{:T(128)}, s32[512]{0:T(512)S(1)}, ...), branch_computations={%region_6.6_spmd, %region_7.9_spmd} | conditional | flops 482209792 | bytes 17717786 | solution.py:78
  308.2 1.9 fusion.26
  316.0 5.9 %conditional.2 = ((f32[112,4,4]{0,2,1:T(4,128)S(1)}, f32[112,4,4]{0,2,1:T(4,128)S(1)}, f32[112,4,4,128]{3,0,2,1:T(8,128)S(1)})) conditional(s32[]{:T(128)} %convert_element_type.61, (f32[112,4,4]{0,2,1:T(4,128)S(1)}, f32[112,4,4]{0,2,1:T(4,128)S(1)}, f32[112,4,4,128]{3,0,2,1:T(8,128)S(1)}) %tuple.67, (s32[]{:T(128)}, s32[512]{0:T(512)S(1)}, ...), branch_computations={%region_6.6_spmd, %region_7.9_spmd} | conditional | flops 482209792 | bytes 17717786 | solution.py:78
  316.0 1.9 fusion.26
  323.8 5.9 %conditional.2 = ((f32[112,4,4]{0,2,1:T(4,128)S(1)}, f32[112,4,4]{0,2,1:T(4,128)S(1)}, f32[112,4,4,128]{3,0,2,1:T(8,128)S(1)})) conditional(s32[]{:T(128)} %convert_element_type.61, (f32[112,4,4]{0,2,1:T(4,128)S(1)}, f32[112,4,4]{0,2,1:T(4,128)S(1)}, f32[112,4,4,128]{3,0,2,1:T(8,128)S(1)}) %tuple.67, (s32[]{:T(128)}, s32[512]{0:T(512)S(1)}, ...), branch_computations={%region_6.6_spmd, %region_7.9_spmd} | conditional | flops 482209792 | bytes 17717786 | solution.py:78
  323.8 1.9 fusion.26
  331.6 5.9 %conditional.2 = ((f32[112,4,4]{0,2,1:T(4,128)S(1)}, f32[112,4,4]{0,2,1:T(4,128)S(1)}, f32[112,4,4,128]{3,0,2,1:T(8,128)S(1)})) conditional(s32[]{:T(128)} %convert_element_type.61, (f32[112,4,4]{0,2,1:T(4,128)S(1)}, f32[112,4,4]{0,2,1:T(4,128)S(1)}, f32[112,4,4,128]{3,0,2,1:T(8,128)S(1)}) %tuple.67, (s32[]{:T(128)}, s32[512]{0:T(512)S(1)}, ...), branch_computations={%region_6.6_spmd, %region_7.9_spmd} | conditional | flops 482209792 | bytes 17717786 | solution.py:78
  331.6 1.9 fusion.26
  339.4 5.9 %conditional.2 = ((f32[112,4,4]{0,2,1:T(4,128)S(1)}, f32[112,4,4]{0,2,1:T(4,128)S(1)}, f32[112,4,4,128]{3,0,2,1:T(8,128)S(1)})) conditional(s32[]{:T(128)} %convert_element_type.61, (f32[112,4,4]{0,2,1:T(4,128)S(1)}, f32[112,4,4]{0,2,1:T(4,128)S(1)}, f32[112,4,4,128]{3,0,2,1:T(8,128)S(1)}) %tuple.67, (s32[]{:T(128)}, s32[512]{0:T(512)S(1)}, ...), branch_computations={%region_6.6_spmd, %region_7.9_spmd} | conditional | flops 482209792 | bytes 17717786 | solution.py:78
  339.4 1.9 fusion.26
  347.2 5.9 %conditional.2 = ((f32[112,4,4]{0,2,1:T(4,128)S(1)}, f32[112,4,4]{0,2,1:T(4,128)S(1)}, f32[112,4,4,128]{3,0,2,1:T(8,128)S(1)})) conditional(s32[]{:T(128)} %convert_element_type.61, (f32[112,4,4]{0,2,1:T(4,128)S(1)}, f32[112,4,4]{0,2,1:T(4,128)S(1)}, f32[112,4,4,128]{3,0,2,1:T(8,128)S(1)}) %tuple.67, (s32[]{:T(128)}, s32[512]{0:T(512)S(1)}, ...), branch_computations={%region_6.6_spmd, %region_7.9_spmd} | conditional | flops 482209792 | bytes 17717786 | solution.py:78
  347.2 1.9 fusion.26
  355.0 5.9 %conditional.2 = ((f32[112,4,4]{0,2,1:T(4,128)S(1)}, f32[112,4,4]{0,2,1:T(4,128)S(1)}, f32[112,4,4,128]{3,0,2,1:T(8,128)S(1)})) conditional(s32[]{:T(128)} %convert_element_type.61, (f32[112,4,4]{0,2,1:T(4,128)S(1)}, f32[112,4,4]{0,2,1:T(4,128)S(1)}, f32[112,4,4,128]{3,0,2,1:T(8,128)S(1)}) %tuple.67, (s32[]{:T(128)}, s32[512]{0:T(512)S(1)}, ...), branch_computations={%region_6.6_spmd, %region_7.9_spmd} | conditional | flops 482209792 | bytes 17717786 | solution.py:78
  355.0 1.9 fusion.26
  362.8 5.9 %conditional.2 = ((f32[112,4,4]{0,2,1:T(4,128)S(1)}, f32[112,4,4]{0,2,1:T(4,128)S(1)}, f32[112,4,4,128]{3,0,2,1:T(8,128)S(1)})) conditional(s32[]{:T(128)} %convert_element_type.61, (f32[112,4,4]{0,2,1:T(4,128)S(1)}, f32[112,4,4]{0,2,1:T(4,128)S(1)}, f32[112,4,4,128]{3,0,2,1:T(8,128)S(1)}) %tuple.67, (s32[]{:T(128)}, s32[512]{0:T(512)S(1)}, ...), branch_computations={%region_6.6_spmd, %region_7.9_spmd} | conditional | flops 482209792 | bytes 17717786 | solution.py:78
  362.8 1.9 fusion.26
  370.6 5.9 %conditional.2 = ((f32[112,4,4]{0,2,1:T(4,128)S(1)}, f32[112,4,4]{0,2,1:T(4,128)S(1)}, f32[112,4,4,128]{3,0,2,1:T(8,128)S(1)})) conditional(s32[]{:T(128)} %convert_element_type.61, (f32[112,4,4]{0,2,1:T(4,128)S(1)}, f32[112,4,4]{0,2,1:T(4,128)S(1)}, f32[112,4,4,128]{3,0,2,1:T(8,128)S(1)}) %tuple.67, (s32[]{:T(128)}, s32[512]{0:T(512)S(1)}, ...), branch_computations={%region_6.6_spmd, %region_7.9_spmd} | conditional | flops 482209792 | bytes 17717786 | solution.py:78
  370.7 1.9 fusion.26
  378.4 5.9 %conditional.2 = ((f32[112,4,4]{0,2,1:T(4,128)S(1)}, f32[112,4,4]{0,2,1:T(4,128)S(1)}, f32[112,4,4,128]{3,0,2,1:T(8,128)S(1)})) conditional(s32[]{:T(128)} %convert_element_type.61, (f32[112,4,4]{0,2,1:T(4,128)S(1)}, f32[112,4,4]{0,2,1:T(4,128)S(1)}, f32[112,4,4,128]{3,0,2,1:T(8,128)S(1)}) %tuple.67, (s32[]{:T(128)}, s32[512]{0:T(512)S(1)}, ...), branch_computations={%region_6.6_spmd, %region_7.9_spmd} | conditional | flops 482209792 | bytes 17717786 | solution.py:78
  378.5 1.9 fusion.26
  386.2 5.9 %conditional.2 = ((f32[112,4,4]{0,2,1:T(4,128)S(1)}, f32[112,4,4]{0,2,1:T(4,128)S(1)}, f32[112,4,4,128]{3,0,2,1:T(8,128)S(1)})) conditional(s32[]{:T(128)} %convert_element_type.61, (f32[112,4,4]{0,2,1:T(4,128)S(1)}, f32[112,4,4]{0,2,1:T(4,128)S(1)}, f32[112,4,4,128]{3,0,2,1:T(8,128)S(1)}) %tuple.67, (s32[]{:T(128)}, s32[512]{0:T(512)S(1)}, ...), branch_computations={%region_6.6_spmd, %region_7.9_spmd} | conditional | flops 482209792 | bytes 17717786 | solution.py:78
  386.3 1.9 fusion.26
  394.0 5.9 %conditional.2 = ((f32[112,4,4]{0,2,1:T(4,128)S(1)}, f32[112,4,4]{0,2,1:T(4,128)S(1)}, f32[112,4,4,128]{3,0,2,1:T(8,128)S(1)})) conditional(s32[]{:T(128)} %convert_element_type.61, (f32[112,4,4]{0,2,1:T(4,128)S(1)}, f32[112,4,4]{0,2,1:T(4,128)S(1)}, f32[112,4,4,128]{3,0,2,1:T(8,128)S(1)}) %tuple.67, (s32[]{:T(128)}, s32[512]{0:T(512)S(1)}, ...), branch_computations={%region_6.6_spmd, %region_7.9_spmd} | conditional | flops 482209792 | bytes 17717786 | solution.py:78
  401.8 5.9 %conditional.2 = ((f32[112,4,4]{0,2,1:T(4,128)S(1)}, f32[112,4,4]{0,2,1:T(4,128)S(1)}, f32[112,4,4,128]{3,0,2,1:T(8,128)S(1)})) conditional(s32[]{:T(128)} %convert_element_type.61, (f32[112,4,4]{0,2,1:T(4,128)S(1)}, f32[112,4,4]{0,2,1:T(4,128)S(1)}, f32[112,4,4,128]{3,0,2,1:T(8,128)S(1)}) %tuple.67, (s32[]{:T(128)}, s32[512]{0:T(512)S(1)}, ...), branch_computations={%region_6.6_spmd, %region_7.9_spmd} | conditional | flops 482209792 | bytes 17717786 | solution.py:78
  401.9 1.9 fusion.26
  409.7 5.9 %conditional.2 = ((f32[112,4,4]{0,2,1:T(4,128)S(1)}, f32[112,4,4]{0,2,1:T(4,128)S(1)}, f32[112,4,4,128]{3,0,2,1:T(8,128)S(1)})) conditional(s32[]{:T(128)} %convert_element_type.61, (f32[112,4,4]{0,2,1:T(4,128)S(1)}, f32[112,4,4]{0,2,1:T(4,128)S(1)}, f32[112,4,4,128]{3,0,2,1:T(8,128)S(1)}) %tuple.67, (s32[]{:T(128)}, s32[512]{0:T(512)S(1)}, ...), branch_computations={%region_6.6_spmd, %region_7.9_spmd} | conditional | flops 482209792 | bytes 17717786 | solution.py:78
  417.5 5.9 %conditional.2 = ((f32[112,4,4]{0,2,1:T(4,128)S(1)}, f32[112,4,4]{0,2,1:T(4,128)S(1)}, f32[112,4,4,128]{3,0,2,1:T(8,128)S(1)})) conditional(s32[]{:T(128)} %convert_element_type.61, (f32[112,4,4]{0,2,1:T(4,128)S(1)}, f32[112,4,4]{0,2,1:T(4,128)S(1)}, f32[112,4,4,128]{3,0,2,1:T(8,128)S(1)}) %tuple.67, (s32[]{:T(128)}, s32[512]{0:T(512)S(1)}, ...), branch_computations={%region_6.6_spmd, %region_7.9_spmd} | conditional | flops 482209792 | bytes 17717786 | solution.py:78
  417.5 1.9 fusion.26
  425.3 5.9 %conditional.2 = ((f32[112,4,4]{0,2,1:T(4,128)S(1)}, f32[112,4,4]{0,2,1:T(4,128)S(1)}, f32[112,4,4,128]{3,0,2,1:T(8,128)S(1)})) conditional(s32[]{:T(128)} %convert_element_type.61, (f32[112,4,4]{0,2,1:T(4,128)S(1)}, f32[112,4,4]{0,2,1:T(4,128)S(1)}, f32[112,4,4,128]{3,0,2,1:T(8,128)S(1)}) %tuple.67, (s32[]{:T(128)}, s32[512]{0:T(512)S(1)}, ...), branch_computations={%region_6.6_spmd, %region_7.9_spmd} | conditional | flops 482209792 | bytes 17717786 | solution.py:78
  425.3 1.9 fusion.26
  433.1 5.9 %conditional.2 = ((f32[112,4,4]{0,2,1:T(4,128)S(1)}, f32[112,4,4]{0,2,1:T(4,128)S(1)}, f32[112,4,4,128]{3,0,2,1:T(8,128)S(1)})) conditional(s32[]{:T(128)} %convert_element_type.61, (f32[112,4,4]{0,2,1:T(4,128)S(1)}, f32[112,4,4]{0,2,1:T(4,128)S(1)}, f32[112,4,4,128]{3,0,2,1:T(8,128)S(1)}) %tuple.67, (s32[]{:T(128)}, s32[512]{0:T(512)S(1)}, ...), branch_computations={%region_6.6_spmd, %region_7.9_spmd} | conditional | flops 482209792 | bytes 17717786 | solution.py:78
  433.1 1.9 fusion.26
  440.9 5.9 %conditional.2 = ((f32[112,4,4]{0,2,1:T(4,128)S(1)}, f32[112,4,4]{0,2,1:T(4,128)S(1)}, f32[112,4,4,128]{3,0,2,1:T(8,128)S(1)})) conditional(s32[]{:T(128)} %convert_element_type.61, (f32[112,4,4]{0,2,1:T(4,128)S(1)}, f32[112,4,4]{0,2,1:T(4,128)S(1)}, f32[112,4,4,128]{3,0,2,1:T(8,128)S(1)}) %tuple.67, (s32[]{:T(128)}, s32[512]{0:T(512)S(1)}, ...), branch_computations={%region_6.6_spmd, %region_7.9_spmd} | conditional | flops 482209792 | bytes 17717786 | solution.py:78
  448.7 5.9 %conditional.2 = ((f32[112,4,4]{0,2,1:T(4,128)S(1)}, f32[112,4,4]{0,2,1:T(4,128)S(1)}, f32[112,4,4,128]{3,0,2,1:T(8,128)S(1)})) conditional(s32[]{:T(128)} %convert_element_type.61, (f32[112,4,4]{0,2,1:T(4,128)S(1)}, f32[112,4,4]{0,2,1:T(4,128)S(1)}, f32[112,4,4,128]{3,0,2,1:T(8,128)S(1)}) %tuple.67, (s32[]{:T(128)}, s32[512]{0:T(512)S(1)}, ...), branch_computations={%region_6.6_spmd, %region_7.9_spmd} | conditional | flops 482209792 | bytes 17717786 | solution.py:78
  456.5 5.9 %conditional.2 = ((f32[112,4,4]{0,2,1:T(4,128)S(1)}, f32[112,4,4]{0,2,1:T(4,128)S(1)}, f32[112,4,4,128]{3,0,2,1:T(8,128)S(1)})) conditional(s32[]{:T(128)} %convert_element_type.61, (f32[112,4,4]{0,2,1:T(4,128)S(1)}, f32[112,4,4]{0,2,1:T(4,128)S(1)}, f32[112,4,4,128]{3,0,2,1:T(8,128)S(1)}) %tuple.67, (s32[]{:T(128)}, s32[512]{0:T(512)S(1)}, ...), branch_computations={%region_6.6_spmd, %region_7.9_spmd} | conditional | flops 482209792 | bytes 17717786 | solution.py:78
  464.3 5.9 %conditional.2 = ((f32[112,4,4]{0,2,1:T(4,128)S(1)}, f32[112,4,4]{0,2,1:T(4,128)S(1)}, f32[112,4,4,128]{3,0,2,1:T(8,128)S(1)})) conditional(s32[]{:T(128)} %convert_element_type.61, (f32[112,4,4]{0,2,1:T(4,128)S(1)}, f32[112,4,4]{0,2,1:T(4,128)S(1)}, f32[112,4,4,128]{3,0,2,1:T(8,128)S(1)}) %tuple.67, (s32[]{:T(128)}, s32[512]{0:T(512)S(1)}, ...), branch_computations={%region_6.6_spmd, %region_7.9_spmd} | conditional | flops 482209792 | bytes 17717786 | solution.py:78
  472.1 5.9 %conditional.2 = ((f32[112,4,4]{0,2,1:T(4,128)S(1)}, f32[112,4,4]{0,2,1:T(4,128)S(1)}, f32[112,4,4,128]{3,0,2,1:T(8,128)S(1)})) conditional(s32[]{:T(128)} %convert_element_type.61, (f32[112,4,4]{0,2,1:T(4,128)S(1)}, f32[112,4,4]{0,2,1:T(4,128)S(1)}, f32[112,4,4,128]{3,0,2,1:T(8,128)S(1)}) %tuple.67, (s32[]{:T(128)}, s32[512]{0:T(512)S(1)}, ...), branch_computations={%region_6.6_spmd, %region_7.9_spmd} | conditional | flops 482209792 | bytes 17717786 | solution.py:78
  479.9 5.9 %conditional.2 = ((f32[112,4,4]{0,2,1:T(4,128)S(1)}, f32[112,4,4]{0,2,1:T(4,128)S(1)}, f32[112,4,4,128]{3,0,2,1:T(8,128)S(1)})) conditional(s32[]{:T(128)} %convert_element_type.61, (f32[112,4,4]{0,2,1:T(4,128)S(1)}, f32[112,4,4]{0,2,1:T(4,128)S(1)}, f32[112,4,4,128]{3,0,2,1:T(8,128)S(1)}) %tuple.67, (s32[]{:T(128)}, s32[512]{0:T(512)S(1)}, ...), branch_computations={%region_6.6_spmd, %region_7.9_spmd} | conditional | flops 482209792 | bytes 17717786 | solution.py:78
  487.7 5.9 %conditional.2 = ((f32[112,4,4]{0,2,1:T(4,128)S(1)}, f32[112,4,4]{0,2,1:T(4,128)S(1)}, f32[112,4,4,128]{3,0,2,1:T(8,128)S(1)})) conditional(s32[]{:T(128)} %convert_element_type.61, (f32[112,4,4]{0,2,1:T(4,128)S(1)}, f32[112,4,4]{0,2,1:T(4,128)S(1)}, f32[112,4,4,128]{3,0,2,1:T(8,128)S(1)}) %tuple.67, (s32[]{:T(128)}, s32[512]{0:T(512)S(1)}, ...), branch_computations={%region_6.6_spmd, %region_7.9_spmd} | conditional | flops 482209792 | bytes 17717786 | solution.py:78
  495.5 5.9 %conditional.2 = ((f32[112,4,4]{0,2,1:T(4,128)S(1)}, f32[112,4,4]{0,2,1:T(4,128)S(1)}, f32[112,4,4,128]{3,0,2,1:T(8,128)S(1)})) conditional(s32[]{:T(128)} %convert_element_type.61, (f32[112,4,4]{0,2,1:T(4,128)S(1)}, f32[112,4,4]{0,2,1:T(4,128)S(1)}, f32[112,4,4,128]{3,0,2,1:T(8,128)S(1)}) %tuple.67, (s32[]{:T(128)}, s32[512]{0:T(512)S(1)}, ...), branch_computations={%region_6.6_spmd, %region_7.9_spmd} | conditional | flops 482209792 | bytes 17717786 | solution.py:78
  503.3 5.9 %conditional.2 = ((f32[112,4,4]{0,2,1:T(4,128)S(1)}, f32[112,4,4]{0,2,1:T(4,128)S(1)}, f32[112,4,4,128]{3,0,2,1:T(8,128)S(1)})) conditional(s32[]{:T(128)} %convert_element_type.61, (f32[112,4,4]{0,2,1:T(4,128)S(1)}, f32[112,4,4]{0,2,1:T(4,128)S(1)}, f32[112,4,4,128]{3,0,2,1:T(8,128)S(1)}) %tuple.67, (s32[]{:T(128)}, s32[512]{0:T(512)S(1)}, ...), branch_computations={%region_6.6_spmd, %region_7.9_spmd} | conditional | flops 482209792 | bytes 17717786 | solution.py:78
  511.1 5.8 %conditional.2 = ((f32[112,4,4]{0,2,1:T(4,128)S(1)}, f32[112,4,4]{0,2,1:T(4,128)S(1)}, f32[112,4,4,128]{3,0,2,1:T(8,128)S(1)})) conditional(s32[]{:T(128)} %convert_element_type.61, (f32[112,4,4]{0,2,1:T(4,128)S(1)}, f32[112,4,4]{0,2,1:T(4,128)S(1)}, f32[112,4,4,128]{3,0,2,1:T(8,128)S(1)}) %tuple.67, (s32[]{:T(128)}, s32[512]{0:T(512)S(1)}, ...), branch_computations={%region_6.6_spmd, %region_7.9_spmd} | conditional | flops 482209792 | bytes 17717786 | solution.py:78
  (402 shorter events, 180.3 us)
Async XLA Ops:
  7.2 4.4 copy-start
  9.2 5.0 copy-start.5
  22.0 7.5 %collective-permute-start = (bf16[1,2,56,1024]{3,2,1,0:T(8,128)(2,1)}, bf16[1,2,56,1024]{3,2,1,0:T(8,128)(2,1)S(1)}, u32[]{:S(2)}, u32[]{:S(2)}) collective-permute-start(bf16[1,2,56,1024]{3,2,1,0:T(8,128)(2,1)} %get-tuple-element.252), channel_id=1, source_target_pairs={{0,16},{16,0},{32,48},{48,32},{64,80},{80,64},{96,112},{112,96},{1... | collective-permute-start | bytes 688136 | tf_op jit(solution)/shard_map/ppermute | solution.py:120
  23.3 22.6 %collective-permute-start.1 = (bf16[1,2,56,1024]{3,2,1,0:T(8,128)(2,1)}, bf16[1,2,56,1024]{3,2,1,0:T(8,128)(2,1)S(1)}, u32[]{:S(2)}, u32[]{:S(2)}) collective-permute-start(bf16[1,2,56,1024]{3,2,1,0:T(8,128)(2,1)} %get-tuple-element.251), channel_id=1, source_target_pairs={{0,32},{16,48},{32,0},{48,16},{64,96},{80,112},{96,64},{112,80},{1... | collective-permute-start | bytes 688136 | tf_op jit(solution)/shard_map/ppermute | solution.py:120
  25.9 21.6 %collective-permute-start.2 = (bf16[1,2,56,1024]{3,2,1,0:T(8,128)(2,1)}, bf16[1,2,56,1024]{3,2,1,0:T(8,128)(2,1)S(1)}, u32[]{:S(2)}, u32[]{:S(2)}) collective-permute-start(bf16[1,2,56,1024]{3,2,1,0:T(8,128)(2,1)} %get-tuple-element.250), channel_id=1, source_target_pairs={{0,48},{16,32},{32,16},{48,0},{64,112},{80,96},{96,80},{112,64},{1... | collective-permute-start | bytes 688136 | tf_op jit(solution)/shard_map/ppermute | solution.py:120
  25.9 24.7 %collective-permute-start.3 = (bf16[1,2,56,1024]{3,2,1,0:T(8,128)(2,1)}, bf16[1,2,56,1024]{3,2,1,0:T(8,128)(2,1)S(1)}, u32[]{:S(2)}, u32[]{:S(2)}) collective-permute-start(bf16[1,2,56,1024]{3,2,1,0:T(8,128)(2,1)} %get-tuple-element.249), channel_id=1, source_target_pairs={{0,64},{16,80},{32,96},{48,112},{64,0},{80,16},{96,32},{112,48},{1... | collective-permute-start | bytes 688136 | tf_op jit(solution)/shard_map/ppermute | solution.py:120
  27.1 24.2 %collective-permute-start.4 = (bf16[1,2,56,1024]{3,2,1,0:T(8,128)(2,1)}, bf16[1,2,56,1024]{3,2,1,0:T(8,128)(2,1)S(1)}, u32[]{:S(2)}, u32[]{:S(2)}) collective-permute-start(bf16[1,2,56,1024]{3,2,1,0:T(8,128)(2,1)} %get-tuple-element.248), channel_id=1, source_target_pairs={{0,80},{16,64},{32,112},{48,96},{64,16},{80,0},{96,48},{112,32},{1... | collective-permute-start | bytes 688136 | tf_op jit(solution)/shard_map/ppermute | solution.py:120
  29.5 28.9 %collective-permute-start.5 = (bf16[1,2,56,1024]{3,2,1,0:T(8,128)(2,1)S(1)}, bf16[1,2,56,1024]{3,2,1,0:T(8,128)(2,1)S(1)}, u32[]{:S(2)}, u32[]{:S(2)}) collective-permute-start(bf16[1,2,56,1024]{3,2,1,0:T(8,128)(2,1)S(1)} %get-tuple-element.247), channel_id=1, source_target_pairs={{0,96},{16,112},{32,64},{48,80},{64,32},{80,48},{96,0},{112,16},{1... | collective-permute-start | bytes 688136 | tf_op jit(solution)/shard_map/ppermute | solution.py:120
  45.9 13.4 %collective-permute-start.6 = (bf16[1,2,56,1024]{3,2,1,0:T(8,128)(2,1)S(1)}, bf16[1,2,56,1024]{3,2,1,0:T(8,128)(2,1)S(1)}, u32[]{:S(2)}, u32[]{:S(2)}) collective-permute-start(bf16[1,2,56,1024]{3,2,1,0:T(8,128)(2,1)S(1)} %get-tuple-element.246), channel_id=1, source_target_pairs={{0,112},{16,96},{32,80},{48,64},{64,48},{80,32},{96,16},{112,0},{1... | collective-permute-start | bytes 688136 | tf_op jit(solution)/shard_map/ppermute | solution.py:120
  47.5 14.4 %collective-permute-start.7 = (bf16[1,2,56,1024]{3,2,1,0:T(8,128)(2,1)S(1)}, bf16[1,2,56,1024]{3,2,1,0:T(8,128)(2,1)S(1)}, u32[]{:S(2)}, u32[]{:S(2)}) collective-permute-start(bf16[1,2,56,1024]{3,2,1,0:T(8,128)(2,1)S(1)} %get-tuple-element.245), channel_id=1, source_target_pairs={{0,128},{16,144},{32,160},{48,176},{64,192},{80,208},{96,224},{112... | collective-permute-start | bytes 688136 | tf_op jit(solution)/shard_map/ppermute | solution.py:120
  50.6 12.0 %collective-permute-start.8 = (bf16[1,2,56,1024]{3,2,1,0:T(8,128)(2,1)S(1)}, bf16[1,2,56,1024]{3,2,1,0:T(8,128)(2,1)S(1)}, u32[]{:S(2)}, u32[]{:S(2)}) collective-permute-start(bf16[1,2,56,1024]{3,2,1,0:T(8,128)(2,1)S(1)} %get-tuple-element.244), channel_id=1, source_target_pairs={{0,144},{16,128},{32,176},{48,160},{64,208},{80,192},{96,240},{112... | collective-permute-start | bytes 688136 | tf_op jit(solution)/shard_map/ppermute | solution.py:120
  51.3 17.9 %collective-permute-start.9 = (bf16[1,2,56,1024]{3,2,1,0:T(8,128)(2,1)S(1)}, bf16[1,2,56,1024]{3,2,1,0:T(8,128)(2,1)S(1)}, u32[]{:S(2)}, u32[]{:S(2)}) collective-permute-start(bf16[1,2,56,1024]{3,2,1,0:T(8,128)(2,1)S(1)} %get-tuple-element.243), channel_id=1, source_target_pairs={{0,160},{16,176},{32,128},{48,144},{64,224},{80,240},{96,192},{112... | collective-permute-start | bytes 688136 | tf_op jit(solution)/shard_map/ppermute | solution.py:120
  58.4 17.1 %collective-permute-start.10 = (bf16[1,2,56,1024]{3,2,1,0:T(8,128)(2,1)S(1)}, bf16[1,2,56,1024]{3,2,1,0:T(8,128)(2,1)S(1)}, u32[]{:S(2)}, u32[]{:S(2)}) collective-permute-start(bf16[1,2,56,1024]{3,2,1,0:T(8,128)(2,1)S(1)} %get-tuple-element.242), channel_id=1, source_target_pairs={{0,176},{16,160},{32,144},{48,128},{64,240},{80,224},{96,208},{112... | collective-permute-start | bytes 688136 | tf_op jit(solution)/shard_map/ppermute | solution.py:120
  59.3 20.6 %collective-permute-start.11 = (bf16[1,2,56,1024]{3,2,1,0:T(8,128)(2,1)S(1)}, bf16[1,2,56,1024]{3,2,1,0:T(8,128)(2,1)S(1)}, u32[]{:S(2)}, u32[]{:S(2)}) collective-permute-start(bf16[1,2,56,1024]{3,2,1,0:T(8,128)(2,1)S(1)} %get-tuple-element.241), channel_id=1, source_target_pairs={{0,192},{16,208},{32,224},{48,240},{64,128},{80,144},{96,160},{112... | collective-permute-start | bytes 688136 | tf_op jit(solution)/shard_map/ppermute | solution.py:120
  61.8 21.8 %collective-permute-start.12 = (bf16[1,2,56,1024]{3,2,1,0:T(8,128)(2,1)S(1)}, bf16[1,2,56,1024]{3,2,1,0:T(8,128)(2,1)S(1)}, u32[]{:S(2)}, u32[]{:S(2)}) collective-permute-start(bf16[1,2,56,1024]{3,2,1,0:T(8,128)(2,1)S(1)} %get-tuple-element.240), channel_id=1, source_target_pairs={{0,208},{16,192},{32,240},{48,224},{64,144},{80,128},{96,176},{112... | collective-permute-start | bytes 688136 | tf_op jit(solution)/shard_map/ppermute | solution.py:120
  62.6 26.0 %collective-permute-start.13 = (bf16[1,2,56,1024]{3,2,1,0:T(8,128)(2,1)S(1)}, bf16[1,2,56,1024]{3,2,1,0:T(8,128)(2,1)S(1)}, u32[]{:S(2)}, u32[]{:S(2)}) collective-permute-start(bf16[1,2,56,1024]{3,2,1,0:T(8,128)(2,1)S(1)} %get-tuple-element.239), channel_id=1, source_target_pairs={{0,224},{16,240},{32,192},{48,208},{64,160},{80,176},{96,128},{112... | collective-permute-start | bytes 688136 | tf_op jit(solution)/shard_map/ppermute | solution.py:120
  69.3 28.8 %collective-permute-start.14 = (bf16[1,2,56,1024]{3,2,1,0:T(8,128)(2,1)S(1)}, bf16[1,2,56,1024]{3,2,1,0:T(8,128)(2,1)S(1)}, u32[]{:S(2)}, u32[]{:S(2)}) collective-permute-start(bf16[1,2,56,1024]{3,2,1,0:T(8,128)(2,1)S(1)} %get-tuple-element.238), channel_id=1, source_target_pairs={{0,240},{16,224},{32,208},{48,192},{64,176},{80,160},{96,144},{112... | collective-permute-start | bytes 688136 | tf_op jit(solution)/shard_map/ppermute | solution.py:120
  107.5 2.7 copy-start.4
  110.2 152.6 %all-gather.2.cloned.1.call-start = ((), (), s32[]{:S(2)}) async-start(), calls=%async_computation | async-start | bytes 31195136 | tf_op jit(solution)/shard_map/all_gather | solution.py:65
  112.5 1.2 copy-start.2
  115.2 183.3 %copy-start.3 = (bf16[1,112,2048]{2,1,0:T(8,128)(2,1)S(1)}, bf16[1,112,2048]{2,1,0:T(8,128)(2,1)}, u32[]{:S(2)}) copy-start(bf16[1,112,2048]{2,1,0:T(8,128)(2,1)} %param.14) | copy-start | bytes 1376260
  516.9 1.6 copy-start.1
Sparse Core Ops, SparseCore 0:
  113.9 148.7 all-gather.1
